TPU v7x, 32 devices: a whole 2x2x4 slice. The times are simulated.
32 devices in a mesh: groups: 2 (over x), seq: 16 (over z, y, core).
Axes of the slice: x: 2, y: 2, z: 4, core: 2. Of those that a mesh axis runs over, the one named last changes fastest.
Arguments:
- hidden: bfloat16 [8192, 2048], P(('groups', 'seq')), parts along dimension 0, may hold values from -6 to 6
- conv_weight: float32 [3, 2048], replicated, may hold values from -1.8 to 1.8
- feat_query_w: bfloat16 [2048, 256], replicated, may hold values from -0.125 to 0.125
- feat_key_w: bfloat16 [2048, 256], replicated, may hold values from -0.125 to 0.125
- win_query: bfloat16 [8192, 2048], P(('groups', 'seq')), parts along dimension 0, may hold values from -48 to 48
- win_key: bfloat16 [8192, 2048], P(('groups', 'seq')), parts along dimension 0, may hold values from -48 to 48
Outputs:
- mixed: bfloat16 [8192, 2048], P(('groups', 'seq')), parts along dimension 0
There are 2 independent parts, one for each index of `groups`. A program takes and returns all parts, laid end to end along the dimension named above; an argument that names none is the same for every part. Nothing has to cross between parts.
All inputs are finite; a program needn't handle non-finite values.
Results may differ from a plain program's by a relative error of at most 0.008.
Values may be sent and summed in bfloat16 or wider, within the bound.
A program may use at most 192 MiB of HBM per device.

v0:
```python
import jax
import jax.numpy as jnp
import numpy as np
from jax import lax
from jax.sharding import PartitionSpec as P

HEADS = 16
FEATURE_DIM = 16
WINDOW = 64


def passed_along(value, axis, steps):
    count = lax.axis_size(axis)
    initial, last = (max(0, -steps), min(count, count - steps))
    return lax.ppermute(value, axis, [(source, source + steps) for source in range(initial, last)])


def carried_in(value, axis, combine, identity):
    peers, index = (lax.axis_size(axis), lax.axis_index(axis))
    everything = jax.tree.map(
        lambda part, kind: lax.all_gather(part.astype(kind), axis),
        value,
        jax.tree.map(lambda a: jnp.bfloat16 if a.dtype == jnp.float32 else a.dtype, value),
    )
    start = jax.tree.map(
        lambda part, zero: jnp.broadcast_to(jnp.asarray(zero, part.dtype), part.shape),
        value,
        identity,
    )

    def lap(k, before):
        reached = k < index
        new = combine(
            before, jax.tree.map(lambda part, own: part[k].astype(own.dtype), everything, value)
        )
        return jax.tree.map(lambda a, b: jnp.where(reached, a, b), new, before)

    return lax.fori_loop(0, peers, lap, start)


def conv_rows(extended, conv_weight):
    wide = extended.astype(jnp.float32)
    total = conv_weight[0] * wide[:-2] + conv_weight[1] * wide[1:-1] + conv_weight[2] * wide[2:]
    return total.astype(jnp.bfloat16)


def taylor(features, heads):
    count = features.shape[0]
    wide = features.astype(jnp.float32).reshape(count, heads, -1)
    width = wide.shape[-1]
    first = wide * width ** (-0.25)
    second = (
        jnp.repeat(wide, width, axis=-1)
        * jnp.tile(wide, (1, 1, width))
        * (width ** (-0.5) / 2.0**0.5)
    )
    ones = jnp.ones((count, heads, 1), jnp.float32)
    return jnp.concatenate([ones, first, second], axis=-1).astype(jnp.bfloat16)


def triangle_tables(width):
    kept = list(range(1 + width))
    where_kept = {}
    for left in range(width):
        for right in range(left, width):
            where_kept[left, right] = len(kept)
            kept.append(1 + width + left * width + right)
    spread = list(range(1 + width))
    for left in range(width):
        for right in range(width):
            spread.append(where_kept[min(left, right), max(left, right)])
    return (np.array(kept, np.int32), np.array(spread, np.int32))


def split_pair(values):
    upper = values.astype(jnp.bfloat16)
    lower = (values - upper.astype(jnp.float32)).astype(jnp.bfloat16)
    return (upper, lower)


def local(hidden, conv_weight, feat_query_w, feat_key_w, win_query, win_key):
    count, width = hidden.shape
    head = width // HEADS
    prev_two = passed_along(hidden[count - 2 :], "seq", 1)
    conv = conv_rows(jnp.concatenate([prev_two, hidden], axis=0), conv_weight)
    val_edge, key_edge = passed_along((conv[count - WINDOW :], win_key[count - WINDOW :]), "seq", 1)
    fq = jnp.dot(conv, feat_query_w, preferred_element_type=jnp.float32).astype(jnp.bfloat16)
    fk = jnp.dot(conv, feat_key_w, preferred_element_type=jnp.float32).astype(jnp.bfloat16)
    local_values = conv.reshape(count, HEADS, head)
    expanded_keys = taylor(fk, HEADS)
    key_value_state = jnp.einsum(
        "jeq,jei->eqi", expanded_keys, local_values, preferred_element_type=jnp.float32
    )
    ksum = jnp.sum(expanded_keys.astype(jnp.float32), axis=0)

    def combine(earlier, later):
        return (earlier[0] + later[0], earlier[1] + later[1])

    kept, spread = triangle_tables(FEATURE_DIM)
    outgoing = (jnp.take(key_value_state, kept, axis=1), jnp.take(ksum, kept, axis=1))
    identity = (jnp.zeros_like(outgoing[0]), jnp.zeros_like(outgoing[1]))
    state, norm = carried_in(outgoing, "seq", combine, identity)
    state = jnp.take(state, spread, axis=1)
    norm = jnp.take(norm, spread, axis=1)
    start = lax.axis_index("seq") * count
    tile = 128
    tiles = count // tile
    keys_ext = jnp.concatenate([key_edge, win_key], axis=0).reshape(count + WINDOW, HEADS, head)
    vals_ext = jnp.concatenate([val_edge, conv], axis=0).reshape(count + WINDOW, HEADS, head)
    key_tiles = jnp.stack(
        [keys_ext[index * tile : index * tile + tile + WINDOW] for index in range(tiles)], axis=0
    )
    val_tiles = jnp.stack(
        [vals_ext[index * tile : index * tile + tile + WINDOW] for index in range(tiles)], axis=0
    )
    queries = win_query.reshape(tiles, tile, HEADS, head)
    scores = jnp.einsum(
        "nqhd,nkhd->nhqk", queries, key_tiles, preferred_element_type=jnp.float32
    ) * head ** (-0.5)
    rows = jnp.arange(tile, dtype=jnp.int32)[:, None]
    cols = jnp.arange(tile + WINDOW, dtype=jnp.int32)[None, :]
    offsets = (jnp.arange(tiles, dtype=jnp.int32) * tile)[:, None, None]
    band = (cols > rows) & (cols <= rows + WINDOW)
    allowed = band[None] & (cols[None] - WINDOW + offsets + start >= 0)
    scores = jnp.where(allowed[:, None], scores, -jnp.inf)
    top = jnp.max(scores, axis=-1, keepdims=True)
    weights = jnp.exp(scores - top)
    probs = (weights / jnp.sum(weights, axis=-1, keepdims=True)).astype(jnp.bfloat16)
    y_win = jnp.einsum(
        "nhqk,nkhd->nqhd", probs, val_tiles, preferred_element_type=jnp.float32
    ).reshape(count, HEADS, head)
    feature_query_head = fq.reshape(count, HEADS, FEATURE_DIM)
    feature_key_head = fk.reshape(count, HEADS, FEATURE_DIM)
    inner_product = jnp.einsum(
        "egz,tgz->get", feature_query_head, feature_key_head, preferred_element_type=jnp.float32
    ) * FEATURE_DIM ** (-0.5)
    taylor_w = 1.0 + inner_product + 0.5 * inner_product * inner_product
    causal = (
        jnp.arange(count, dtype=jnp.int32)[None, :] <= jnp.arange(count, dtype=jnp.int32)[:, None]
    )
    taylor_w = jnp.where(causal[None], taylor_w, 0.0)
    den_in = jnp.sum(taylor_w, axis=-1)
    num_in = jnp.einsum(
        "hqk,khd->qhd",
        taylor_w.astype(jnp.bfloat16),
        local_values,
        preferred_element_type=jnp.float32,
    )
    phq = taylor(fq, HEADS)
    state_upper, state_lower = split_pair(state)
    both_states = jnp.concatenate([state_upper, state_lower], axis=2)
    both_out = jnp.einsum("qhf,hfd->qhd", phq, both_states, preferred_element_type=jnp.float32)
    num_out = both_out[..., :head] + both_out[..., head:]
    norm_upper, norm_lower = split_pair(norm)
    den_out = jnp.einsum(
        "qhf,hf->qh", phq, norm_upper, preferred_element_type=jnp.float32
    ) + jnp.einsum("qhf,hf->qh", phq, norm_lower, preferred_element_type=jnp.float32)
    y_lin = (num_in + num_out) / (den_in.T + den_out)[..., None]
    return (y_win + y_lin).reshape(count, width).astype(jnp.bfloat16)


def solution(mesh):
    placed = (
        P(("groups", "seq"), None),
        P(),
        P(),
        P(),
        P(("groups", "seq"), None),
        P(("groups", "seq"), None),
    )
    return jax.shard_map(
        local, mesh=mesh, in_specs=placed, out_specs=P(("groups", "seq"), None), check_vma=False
    )
```

profile of v0, /device:TPU:0, one launch (start us, length us, event | category | flops | bytes accessed | tf_op | source)
XLA Modules:
  0.0 178.6 jit_solution(12560193133600437837)
XLA Ops:
  7.4 2.4 %collective-permute-start = (bf16[2,2048]{1,0:T(2,128)(2,1)S(1)}, bf16[2,2048]{1,0:T(2,128)(2,1)S(1)}, u32[]{:S(2)}, u32[]{:S(2)}) collective-permute-start(bf16[2,2048]{1,0:T(2,128)(2,1)S(1)} %slice.52), channel_id=1, source_target_pairs={{0,1},{1,2},{2,3},{3,4},{4,5},{5,6},{6,7},{7,8},{8,9},{9,10},{10,1... | collective-permute-start | bytes 24584 | tf_op jit(solution)/shard_map/ppermute | solution.py:15
  11.4 1.5 maximum_convert_fusion
  16.9 1.6 gather_fusion
  19.3 5.2 %collective-permute-start.2 = (bf16[64,2048]{1,0:T(8,128)(2,1)}, bf16[64,2048]{1,0:T(8,128)(2,1)}, u32[]{:S(2)}, u32[]{:S(2)}) collective-permute-start(bf16[64,2048]{1,0:T(8,128)(2,1)} %slice.61), channel_id=1, source_target_pairs={{0,1},{1,2},{2,3},{3,4},{4,5},{5,6},{6,7},{7,8},{8,9},{9,10},{10,1... | collective-permute-start | bytes 786440 | tf_op jit(solution)/shard_map/ppermute | solution.py:15
  24.5 2.4 %copy.62 = bf16[32,8,16,128]{3,2,1,0:T(8,128)(2,1)} copy(bf16[32,8,16,128]{3,1,2,0:T(8,128)(2,1)} %bitcast.138) | data formatting | bytes 2097152
  27.0 1.3 pad_clamp_fusion
  30.4 3.3 %convert_reduce_fusion = bf16[16,273]{1,0:T(8,128)(2,1)} fusion(bf16[256,16,256]{0,2,1:T(8,128)(2,1)} %bitcast.127, bf16[256,16,16]{0,2,1:T(8,128)(2,1)} %copy-done.12, bf16[273]{0:T(512)(128)(2,1)} %copy-done.18), kind=kLoop, calls=%fused_computation.9 | loop fusion | flops 7823088 | bytes 2237506 | tf_op jit(solution)/shard_map/reduce_sum | solution.py:94
  33.7 1.4 copy.43
  35.2 2.3 %gather_fusion.1 = bf16[153,16]{1,0:T(8,128)(2,1)} fusion(bf16[16,273]{0,1:T(8,128)(2,1)} %copy.43, s32[1024]{0:T(1024)} %copy-done.20), kind=kCustom, calls=%fused_computation.1 | custom fusion | bytes 10404 | tf_op jit(solution)/shard_map/jit(_take)/gather | solution.py:100
  37.5 1.4 copy.44
  38.9 2.7 %collective-permute-start.1 = (bf16[64,2048]{1,0:T(8,128)(2,1)}, bf16[64,2048]{1,0:T(8,128)(2,1)S(1)}, u32[]{:S(2)}, u32[]{:S(2)}) collective-permute-start(bf16[64,2048]{1,0:T(8,128)(2,1)} %slice.77), channel_id=1, source_target_pairs={{0,1},{1,2},{2,3},{3,4},{4,5},{5,6},{6,7},{7,8},{8,9},{9,10},{10,1... | collective-permute-start | bytes 786440 | tf_op jit(solution)/shard_map/ppermute | solution.py:15
  41.6 27.4 %all-gather.1 = bf16[256,153]{1,0:T(8,128)(2,1)} all-gather(bf16[16,153]{1,0:T(8,128)(2,1)} %copy.44), channel_id=3, replica_groups=mesh['groups'=2,'seq'=16] {'seq'}, dimensions={0}, use_global_device_ids=true | all-gather | bytes 83232 | tf_op jit(solution)/shard_map/all_gather | solution.py:21
  69.0 1.8 %convolution_convert_fusion.1 = bf16[256,256]{0,1:T(8,128)(2,1)S(1)} fusion(bf16[256,2048]{1,0:T(8,128)(2,1)S(1)} %fusion.18, bf16[2048,256]{1,0:T(8,128)(2,1)} %param.12), kind=kOutput, calls=%fused_computation.59 | convolution fusion | flops 268500992 | bytes 2228224 | tf_op jit(solution)/shard_map/dot_general | solution.py:87
  71.6 3.9 %fusion.1 = (f32[16,256]{1,0:T(8,128)}, f32[16,256,256]{1,2,0:T(8,128)}) fusion(pred[256,256]{0,1:T(8,128)(4,1)S(1)} %copy-done.13, bf16[256,16,16]{0,2,1:T(8,128)(2,1)S(1)} %bitcast.137, bf16[256,16,16]{0,2,1:T(8,128)(2,1)S(1)} %bitcast.136), kind=kOutput, calls=%fused_computation.16 | convolution fusion | flops 40890368 | bytes 4538368 | tf_op jit(solution)/shard_map/egz,tgz->get/dot_general | solution.py:134
  75.5 2.6 %pad_maximum_fusion.1 = bf16[256,16,273]{0,2,1:T(8,128)(2,1)} fusion(bf16[256,16,256]{0,2,1:T(8,128)(2,1)S(1)} %bitcast.125, bf16[256,16,16]{0,2,1:T(8,128)(2,1)S(1)} %multiply_convert_fusion.2, bf16[273]{0:T(512)(128)(2,1)S(1)} %copy-done.19), kind=kLoop, calls=%fused_computation.24 | loop fusion | flops 6709248 | bytes 4465186 | tf_op jit(solution)/shard_map/concatenate | solution.py:58
  84.3 2.5 %copy.38 = f32[2,128,16,128]{3,2,1,0:T(8,128)} copy(f32[2,128,16,128]{3,1,2,0:T(8,128)S(1)} %convolution_bitcast_fusion) | data formatting | bytes 4194304 | tf_op jit(solution)/shard_map/nhqk,nkhd->nqhd/transpose | solution.py:129
  86.9 3.0 %copy.49 = f32[256,16,128]{0,2,1:T(8,128)} copy(f32[256,16,128]{2,1,0:T(8,128)} %bitcast.128) | data formatting | bytes 4194304 | tf_op jit(solution)/shard_map/reshape | solution.py:131
  89.8 23.6 %all-gather.4.cloned.1.call-done = bf16[256,153,128]{2,0,1:T(8,128)(2,1)} async-done(((bf16[16,153,128]{2,0,1:T(8,128)(2,1)}), bf16[256,153,128]{2,0,1:T(8,128)(2,1)}) %all-gather.4.cloned.1.call-update) | async-done | bytes 10027024 | tf_op jit(solution)/shard_map/all_gather | solution.py:21
  113.4 38.8 %while.16 = (s32[]{:T(128)}, f32[16,153,128]{2,1,0:T(8,128)S(1)}, f32[16,153]{1,0:T(8,128)S(1)}, s32[]{:T(128)}, bf16[16,16,153,128]{3,1,0,2:T(8,128)(2,1)}, /*i...) while((s32[]{:T(128)}, f32[16,153,128]{2,1,0:T(8,128)S(1)}, f32[16,153]{1,0:T(8,128)S(1)}, ...), condition=%wide.region_4.5_spmd.clone, body=%wide.region_3.4_spmd.clone.sunk | while | flops 1263172 | bytes 4411411 | solution.py:38
  113.4 1.2 constant_dynamic-slice_fusion.2
  115.8 1.2 constant_dynamic-slice_fusion.2
  118.3 1.2 constant_dynamic-slice_fusion.2
  120.7 1.2 constant_dynamic-slice_fusion.2
  153.4 1.8 %copy.46 = f32[16,153,128]{2,0,1:T(8,128)} copy(f32[16,153,128]{2,1,0:T(8,128)S(1)} %get-tuple-element.115) | data formatting | bytes 2506752 | tf_op jit(solution)/shard_map/while | solution.py:38
  155.2 2.1 %gather_fusion.2 = f32[273,16,128]{2,1,0:T(8,128)S(1)} fusion(f32[16,153,128]{2,0,1:T(8,128)} %copy.46, s32[1024]{0:T(1024)S(1)} %copy-done.16), kind=kCustom, calls=%fused_computation.2 | custom fusion | bytes 4473924 | tf_op jit(solution)/shard_map/jit(_take)/gather | solution.py:103
  157.3 1.4 copy-done.3
  158.7 1.7 copy.84
  160.4 3.5 %fusion.8 = bf16[16,273,128]{2,1,0:T(8,128)(2,1)} fusion(f32[273,16,128]{2,1,0:T(8,128)} %copy-done.3), kind=kLoop, calls=%fused_computation.27 | loop fusion | flops 2236416 | bytes 3354624 | tf_op jit(solution)/shard_map/convert_element_type | solution.py:77
  165.9 1.4 fusion.9
  167.7 1.3 copy-done.21
  169.0 1.3 fusion.24
  170.4 1.4 copy.50
  (139 shorter events, 53.4 us)
Async XLA Ops:
  6.5 7.0 %copy-start = (bf16[2048,256]{1,0:T(8,128)(2,1)S(1)}, bf16[2048,256]{1,0:T(8,128)(2,1)}, u32[]{:S(2)}) copy-start(bf16[2048,256]{1,0:T(8,128)(2,1)} %param.13) | copy-start | bytes 3145732
  6.5 106.9 %all-gather.4.cloned.1.call-start = ((), (), s32[]{:S(2)}) async-start(), calls=%async_computation | async-start | bytes 10653696 | tf_op jit(solution)/shard_map/all_gather | solution.py:21
  7.4 4.0 %collective-permute-start = (bf16[2,2048]{1,0:T(2,128)(2,1)S(1)}, bf16[2,2048]{1,0:T(2,128)(2,1)S(1)}, u32[]{:S(2)}, u32[]{:S(2)}) collective-permute-start(bf16[2,2048]{1,0:T(2,128)(2,1)S(1)} %slice.52), channel_id=1, source_target_pairs={{0,1},{1,2},{2,3},{3,4},{4,5},{5,6},{6,7},{7,8},{8,9},{9,10},{10,1... | collective-permute-start | bytes 24584 | tf_op jit(solution)/shard_map/ppermute | solution.py:15
  11.4 5.6 %copy-start.20 = (s32[1024]{0:T(1024)}, s32[1024]{0:T(1024)S(1)}, u32[]{:S(2)}) copy-start(s32[1024]{0:T(1024)S(1)} %pad_clamp_fusion.1) | copy-start | bytes 12292
  11.4 4.1 %copy-start.18 = (bf16[273]{0:T(512)(128)(2,1)}, bf16[273]{0:T(512)(128)(2,1)S(1)}, u32[]{:S(2)}) copy-start(bf16[273]{0:T(512)(128)(2,1)S(1)} %pad.5.clone) | copy-start | bytes 1642
  14.2 1.3 copy-start.12
  14.9 1.6 copy-start.10
  15.5 1.3 copy-start.4
  16.8 1.8 %copy-start.7 = (bf16[256,2048]{1,0:T(8,128)(2,1)S(1)}, bf16[256,2048]{1,0:T(8,128)(2,1)}, u32[]{:S(2)}) copy-start(bf16[256,2048]{1,0:T(8,128)(2,1)} %param.15) | copy-start | bytes 3145732
  19.3 58.8 %collective-permute-start.2 = (bf16[64,2048]{1,0:T(8,128)(2,1)}, bf16[64,2048]{1,0:T(8,128)(2,1)}, u32[]{:S(2)}, u32[]{:S(2)}) collective-permute-start(bf16[64,2048]{1,0:T(8,128)(2,1)} %slice.61), channel_id=1, source_target_pairs={{0,1},{1,2},{2,3},{3,4},{4,5},{5,6},{6,7},{7,8},{8,9},{9,10},{10,1... | collective-permute-start | bytes 786440 | tf_op jit(solution)/shard_map/ppermute | solution.py:15
  38.9 43.7 %collective-permute-start.1 = (bf16[64,2048]{1,0:T(8,128)(2,1)}, bf16[64,2048]{1,0:T(8,128)(2,1)S(1)}, u32[]{:S(2)}, u32[]{:S(2)}) collective-permute-start(bf16[64,2048]{1,0:T(8,128)(2,1)} %slice.77), channel_id=1, source_target_pairs={{0,1},{1,2},{2,3},{3,4},{4,5},{5,6},{6,7},{7,8},{8,9},{9,10},{10,1... | collective-permute-start | bytes 786440 | tf_op jit(solution)/shard_map/ppermute | solution.py:15
  69.0 2.5 %copy-start.13 = (pred[256,256]{0,1:T(8,128)(4,1)S(1)}, pred[256,256]{0,1:T(8,128)(4,1)}, u32[]{:S(2)}) copy-start(pred[256,256]{0,1:T(8,128)(4,1)} %iota_compare_fusion) | copy-start | bytes 196612
  71.6 3.9 %copy-start.19 = (bf16[273]{0:T(512)(128)(2,1)S(1)}, bf16[273]{0:T(512)(128)(2,1)}, u32[]{:S(2)}) copy-start(bf16[273]{0:T(512)(128)(2,1)} %copy-done.18) | copy-start | bytes 1642
  79.5 1.2 copy-start.8
  80.7 0.8 copy-start.15
  113.4 38.9 %copy-start.16 = (s32[1024]{0:T(1024)S(1)}, s32[1024]{0:T(1024)}, u32[]{:S(2)}) copy-start(s32[1024]{0:T(1024)} %pad_clamp_fusion) | copy-start | bytes 12292
  157.3 1.4 copy-start.3
  160.4 3.8 %copy-start.2 = (bf16[256,16,273]{0,2,1:T(8,128)(2,1)S(1)}, bf16[256,16,273]{0,2,1:T(8,128)(2,1)}, u32[]{:S(2)}) copy-start(bf16[256,16,273]{0,2,1:T(8,128)(2,1)} %pad_maximum_fusion.1) | copy-start | bytes 6709252
  164.3 1.3 copy-start.5
  164.3 1.6 copy-start.6
  165.9 1.4 copy-start.17
  165.9 1.6 copy-start.9
  165.9 1.9 %copy-start.11 = (bf16[32,16,8,128]{3,2,1,0:T(8,128)(2,1)S(1)}, bf16[32,16,8,128]{3,2,1,0:T(8,128)(2,1)}, u32[]{:S(2)}) copy-start(bf16[32,16,8,128]{3,2,1,0:T(8,128)(2,1)} %copy-done.10) | copy-start | bytes 3145732
  165.9 1.9 %copy-start.14 = (pred[256,256]{0,1:T(8,128)(4,1)S(1)}, pred[256,256]{0,1:T(8,128)(4,1)}, u32[]{:S(2)}) copy-start(pred[256,256]{0,1:T(8,128)(4,1)} %iota_compare_fusion) | copy-start | bytes 196612
  165.9 3.2 %copy-start.21 = (f32[16,256,256]{1,2,0:T(8,128)S(1)}, f32[16,256,256]{1,2,0:T(8,128)}, u32[]{:S(2)}) copy-start(f32[16,256,256]{1,2,0:T(8,128)} %get-tuple-element.178) | copy-start | bytes 12582916
  169.0 2.8 %copy-start.1 = (bf16[2048,256]{1,0:T(8,128)(2,1)S(1)}, bf16[2048,256]{1,0:T(8,128)(2,1)}, u32[]{:S(2)}) copy-start(bf16[2048,256]{1,0:T(8,128)(2,1)} %param.13) | copy-start | bytes 3145732
Sparse Core Ops, SparseCore 0:
  18.7 94.6 all-gather.3
where the time goes:
time: 181 us; the launch traced here: 179 us
  local copies, waits for them, and re-layouts  52 us (29%)
  other arithmetic  38.9 us (21%)
  blocking collectives  27.4 us (15%)
  waiting for transfers between devices  23.6 us (13%)
  between operations  13.9 us (8%)
  matrix products  12.4 us (7%)
  starting transfers between devices  10.3 us (6%)
    all_gather x1, blocking collectives, carried_in(): lax.all_gather(part.astype(kind), axis)  27.4 us
    all_gather x1, waiting for transfers between devices, carried_in(): lax.all_gather(part.astype(kind), axis)  23.6 us
    select_n x32, other arithmetic, lap(): return jax.tree.map(lambda a, b: jnp.where(reached, a, b), new, before)  19.3 us
    dynamic_slice x16, local copies, waits for them, and re-layouts, lap(): part[k].astype(own.dtype)  19.3 us
    ppermute x3, starting transfers between devices, passed_along(): lax.ppermute(value, axis, [(source, source + steps) for source in range(i...  10.3 us
    unnamed x49, local copies, waits for them, and re-layouts  7.83 us
    dot_general x1, matrix products, local(): jnp.einsum('egz,tgz->get', feature_query_head, feature_key_head, preferre...  3.9 us
    gather x2, local copies, waits for them, and re-layouts, local(): state = jnp.take(state, spread, axis=1)  3.82 us
  transfers between devices with their start and end apart: 4, of which 1 were waited for; matrix products, arithmetic and copies ran while one was open for 21% of the time, Pallas kernels for 0%

commit v1 on v0

v1 whole, which is shorter than its diff:
```python
import functools

import jax
import jax.numpy as jnp
import numpy as np
from jax import lax
from jax.experimental import pallas as pl
from jax.experimental.pallas import tpu as pltpu
from jax.sharding import PartitionSpec as P

HEADS = 16
FEAT = 16
WINDOW = 64
TEAM = 4
ROWS = 160
QUADS = 136
C2 = (FEAT**-0.5) / 2.0**0.5
BF = jnp.bfloat16
F32 = jnp.float32


def tables(block):
    pairs = [(i, j) for i in range(FEAT) for j in range(i, FEAT)]
    left_k = np.zeros((2 * ROWS, 2 * FEAT), np.float32)
    reps = block // FEAT
    sel_q = np.zeros((FEAT, 512), np.float32)
    rows_q = np.zeros((8, 256), np.float32)
    for f, (i, j) in enumerate(pairs):
        left_k[f, i] = 1.0
        left_k[ROWS + f, j] = 1.0
        sel_q[i, f] = 1.0
        sel_q[j, 256 + f] = 1.0
        rows_q[2, f] = np.float32(C2) * (1.0 if i == j else 2.0)
    for i in range(FEAT):
        f = QUADS + i
        left_k[f, i] = 1.0
        left_k[ROWS + f, FEAT] = 0.5
        sel_q[i, f] = 1.0
        rows_q[1, f] = 0.5
        rows_q[2, f] = 1.0
    f = QUADS + FEAT
    left_k[f, FEAT] = 1.0
    left_k[ROWS + f, FEAT] = 1.0
    rows_q[0, f] = 1.0
    rows_q[1, f] = 1.0
    rows_q[2, f] = 1.0
    return jnp.asarray(left_k, BF), jnp.asarray(np.tile(sel_q, (reps, 1)), BF), jnp.asarray(rows_q, F32)


def nt(a, b):
    return lax.dot_general(a, b, (((1,), (1,)), ((), ())), preferred_element_type=F32)


def nn(a, b):
    return jnp.dot(a, b, preferred_element_type=F32)


def kernel(
    n, hid, cw, wq, wk, qry, key, selk, selq, rowq, out,
    hprev, kprev, vprev, cv, fqs, fkt, st, rbuf, total, cin, cout, obuf, sbuf,
    ywin, num, den, wbias, cmask,
    hs_send, hs_recv, a_send, a_recv, c_send, c_recv, b_send, b_recv,
):
    count, width = hid.shape
    head = width // HEADS
    per = HEADS // TEAM
    me = lax.axis_index("seq")
    team = me // TEAM
    pos = lax.rem(me, TEAM)
    teams = n // TEAM
    has_prev, has_next = me > 0, me < n - 1
    has_up, has_down = team > 0, team < teams - 1
    base_dev = team * TEAM

    def peer(d):
        return base_dev + lax.rem(pos + d, TEAM)

    barrier = pltpu.get_barrier_semaphore()

    def hello(dev):
        pl.semaphore_signal(barrier, inc=1, device_id={"seq": dev}, device_id_type=pl.DeviceIdType.MESH)

    for d in range(1, TEAM):
        hello(peer(d))
    pl.when(has_prev)(lambda: hello(me - 1))
    pl.when(has_next)(lambda: hello(me + 1))
    pl.when(has_up)(lambda: hello(me - TEAM))
    pl.when(has_down)(lambda: hello(me + TEAM))
    greeted = TEAM - 1
    for there in (has_prev, has_next, has_up, has_down):
        greeted = greeted + there.astype(jnp.int32)
    pl.semaphore_wait(barrier, greeted)

    def remote(src, dst, send, recv, dev):
        return pltpu.make_async_remote_copy(
            src_ref=src, dst_ref=dst, send_sem=send, recv_sem=recv,
            device_id={"seq": dev}, device_id_type=pl.DeviceIdType.MESH,
        )

    tail_copy = remote(hid.at[pl.ds(count - 16, 16)], hprev, hs_send.at[0], hs_recv.at[0], me + 1)
    key_copy = remote(key.at[pl.ds(count - WINDOW, WINDOW)], kprev, hs_send.at[1], hs_recv.at[1], me + 1)
    val_copy = remote(cv.at[pl.ds(count - WINDOW, WINDOW)], vprev, hs_send.at[2], hs_recv.at[2], me + 1)

    @pl.when(has_next)
    def _():
        tail_copy.start()
        key_copy.start()

    @pl.when(jnp.logical_not(has_prev))
    def _():
        hprev[...] = jnp.zeros_like(hprev)
        kprev[...] = jnp.zeros_like(kprev)
        vprev[...] = jnp.zeros_like(vprev)

    r = lax.broadcasted_iota(jnp.int32, (count, head), 0)
    j = lax.broadcasted_iota(jnp.int32, (count, head), 1)
    rr = lax.rem(r, WINDOW)
    first = jnp.where(has_prev, 0, WINDOW)
    ok = (j > rr) & (j <= rr + WINDOW) & ((j >= first) | (r >= WINDOW))
    wbias[...] = jnp.where(ok, 0.0, -1e30)
    r = lax.broadcasted_iota(jnp.int32, (count, count), 0)
    j = lax.broadcasted_iota(jnp.int32, (count, count), 1)
    cmask[...] = jnp.where(j <= r, 1.0, 0.0)

    pl.when(has_prev)(lambda: tail_copy.wait_recv())

    row = lax.broadcasted_iota(jnp.int32, (count, head), 0)

    def conv_step(b, c):
        cols = pl.ds(pl.multiple_of(b * head, head), head)
        h = hid[:, cols].astype(F32)
        hp = hprev[:, cols].astype(F32)
        w = cw[:, cols]
        h1 = jnp.where(row == 0, hp[15:16], pltpu.roll(h, 1, 0))
        h2 = jnp.where(row == 0, hp[14:15], jnp.where(row == 1, hp[15:16], pltpu.roll(h, 2, 0)))
        cv[:, cols] = (w[0:1] * h2 + w[1:2] * h1 + w[2:3] * h).astype(BF)
        return c

    lax.fori_loop(0, HEADS, conv_step, 0)
    pl.when(has_next)(lambda: val_copy.start())

    fk = nn(cv[...], wk[...]).astype(BF).astype(F32)
    fkt[...] = fk.T.astype(BF)

    trow = lax.broadcasted_iota(jnp.int32, (16, count), 0)
    pick_a = jnp.where(trow == 9, 1.0, 0.0).astype(BF)
    pick_b = jnp.where(trow == 10, 1.0, 0.0).astype(BF)
    ones_k = jnp.ones((FEAT, count), BF)
    zeros_k = jnp.zeros((256 - ROWS, count), BF)

    def state_step(h, c):
        x = jnp.concatenate([fkt[pl.ds(pl.multiple_of(h * FEAT, FEAT), FEAT), :], ones_k], axis=0)
        ab = nn(selk[...], x)
        p = ab[:ROWS] * ab[ROWS:]
        p = jnp.concatenate([p[:QUADS] * C2, p[QUADS:]], axis=0).astype(BF)
        v = cv[:, pl.ds(pl.multiple_of(h * head, head), head)]
        s = nn(p, v)
        tail = s[144:] + nt(pick_a, p[:128]) + nt(pick_b, jnp.concatenate([p[128:], zeros_k], axis=0))
        st[h] = jnp.concatenate([s[:144], tail], axis=0).astype(BF)
        return c

    a_copies = []
    for d in range(1, TEAM):
        p_d = lax.rem(pos + d, TEAM)
        lax.fori_loop(0, per, lambda k, c, p_d=p_d: state_step(p_d * per + k, c), 0)
        copy = remote(st.at[pl.ds(p_d * per, per)], rbuf.at[pos], a_send.at[d], a_recv.at[d], peer(d))
        copy.start()
        a_copies.append(copy)
    lax.fori_loop(0, per, lambda k, c: state_step(pos * per + k, c), 0)

    fq = nn(cv[...], wq[...]).astype(BF)
    for b in range(2):
        fqs[b] = fq[:, b * 128 : (b + 1) * 128]

    ones_v = jnp.ones((count, head), BF)
    lane = lax.broadcasted_iota(jnp.int32, (8, 128), 1)

    def masked_query(h):
        mask = jnp.where(lane // FEAT == lax.rem(h, 8), 1.0, 0.0)[0:1].astype(BF)
        return fqs[h // 8] * mask

    def local_step(h, c):
        cols = pl.ds(pl.multiple_of(h * head, head), head)
        q = qry[:, cols]
        k = jnp.concatenate([kprev[:, cols], key[:, cols]], axis=0)
        v = cv[:, cols]
        ve = jnp.concatenate([vprev[:, cols], v], axis=0)
        s = jnp.concatenate(
            [nt(q[i : i + WINDOW], k[i : i + 2 * WINDOW]) for i in range(0, count, WINDOW)], axis=0
        )
        s = s * head**-0.5 + wbias[...]
        w = jnp.exp(s - jnp.max(s, axis=-1, keepdims=True)).astype(BF)
        va = jnp.concatenate([ve, jnp.ones_like(ve)], axis=1)
        y = jnp.concatenate(
            [nn(w[i : i + WINDOW], va[i : i + 2 * WINDOW]) for i in range(0, count, WINDOW)], axis=0
        )
        ywin[:, cols] = y[:, :head] / y[:, head:]
        fqm = masked_query(h)
        x = nn(fqm, fkt[pl.ds(pl.multiple_of((h // 8) * 128, 128), 128), :]) * FEAT**-0.5
        a = ((1.0 + x + 0.5 * x * x) * cmask[...]).astype(BF)
        na = nn(a, jnp.concatenate([v, ones_v], axis=1))
        num[:, cols] = na[:, :head]
        den[:, cols] = na[:, head:]
        return c

    def collect():
        rbuf[pos] = st[pl.ds(pos * per, per)]
        for copy in a_copies:
            copy.wait_recv()
        total[...] = (
            rbuf[0].astype(F32) + rbuf[1].astype(F32) + rbuf[2].astype(F32) + rbuf[3].astype(F32)
        )

    chain = remote(cout, cin, c_send, c_recv, me + TEAM)
    b_copies = [
        remote(obuf.at[d], sbuf.at[pos], b_send.at[d], b_recv.at[d], peer(d)) for d in range(1, TEAM)
    ]

    def pass_on():
        pl.when(has_up)(lambda: chain.wait_recv())

        @pl.when(jnp.logical_not(has_up))
        def _():
            cin[...] = jnp.zeros_like(cin)

        @pl.when(has_down)
        def _():
            cout[...] = (cin[...].astype(F32) + total[...]).astype(BF)
            chain.start()

        base = cin[...].astype(F32)
        for d in range(TEAM):
            target = lax.rem(pos + d, TEAM)
            acc = base
            for i in range(TEAM - 1):
                acc = acc + rbuf[i].astype(F32) * jnp.where(i < target, 1.0, 0.0)
            if d == 0:
                sbuf[pos] = acc.astype(BF)
            else:
                obuf[d] = acc.astype(BF)
                b_copies[d - 1].start()

    pl.when(has_prev)(lambda: key_copy.wait_recv())
    pl.when(has_prev)(lambda: val_copy.wait_recv())
    lax.fori_loop(0, 4, local_step, 0)
    collect()
    turn = jnp.minimum(4 + 4 * team, HEADS - 1)

    def local_and_pass(h, c):
        pl.when(h == turn)(pass_on)
        return local_step(h, c)

    lax.fori_loop(4, HEADS, local_and_pass, 0)
    for copy in b_copies:
        copy.wait_recv()

    spare = jnp.zeros((256 - ROWS, head), BF)

    def final_step(h, c):
        cols = pl.ds(pl.multiple_of(h * head, head), head)
        lr = nn(masked_query(h), selq[...])
        ph = (((lr[:, :256] + rowq[0:1]) * (lr[:, 256:] + rowq[1:2])) * rowq[2:3]).astype(BF)
        s = sbuf[h // per, lax.rem(h, per)]
        t = s[144:].astype(F32)
        nrow = jnp.concatenate(
            [jnp.broadcast_to(t[9:10], (head, head)), jnp.broadcast_to(t[10:11], (head, head))], axis=1
        ).astype(BF)
        no = nn(ph, jnp.concatenate([s, spare], axis=0))
        do = nt(ph, nrow)
        y = ywin[:, cols] + (num[:, cols] + no) / (den[:, cols] + do)
        out[:, cols] = y.astype(BF)
        return c

    lax.fori_loop(0, HEADS, final_step, 0)

    @pl.when(has_next)
    def _():
        tail_copy.wait_send()
        key_copy.wait_send()
        val_copy.wait_send()

    for copy in a_copies + b_copies:
        copy.wait_send()
    pl.when(has_down)(lambda: chain.wait_send())


def local(n, hidden, conv_weight, feat_query_w, feat_key_w, win_query, win_key):
    count, width = hidden.shape
    head = width // HEADS
    per = HEADS // TEAM
    selk, selq, rowq = tables(128)
    quarter = (per, ROWS, head)
    dma = pltpu.SemaphoreType.DMA
    return pl.pallas_call(
        functools.partial(kernel, n),
        out_shape=jax.ShapeDtypeStruct((count, width), BF),
        in_specs=[pl.BlockSpec(memory_space=pltpu.VMEM)] * 9,
        out_specs=pl.BlockSpec(memory_space=pltpu.VMEM),
        scratch_shapes=[
            pltpu.VMEM((16, width), BF),
            pltpu.VMEM((WINDOW, width), BF),
            pltpu.VMEM((WINDOW, width), BF),
            pltpu.VMEM((count, width), BF),
            pltpu.VMEM((2, count, 128), BF),
            pltpu.VMEM((256, count), BF),
            pltpu.VMEM((HEADS, ROWS, head), BF),
            pltpu.VMEM((TEAM,) + quarter, BF),
            pltpu.VMEM(quarter, F32),
            pltpu.VMEM(quarter, BF),
            pltpu.VMEM(quarter, BF),
            pltpu.VMEM((TEAM,) + quarter, BF),
            pltpu.VMEM((TEAM,) + quarter, BF),
            pltpu.VMEM((count, width), F32),
            pltpu.VMEM((count, width), F32),
            pltpu.VMEM((count, width), F32),
            pltpu.VMEM((count, head), F32),
            pltpu.VMEM((count, count), F32),
            dma((3,)), dma((3,)), dma((TEAM,)), dma((TEAM,)), dma, dma, dma((TEAM,)), dma((TEAM,)),
        ],
        compiler_params=pltpu.CompilerParams(
            collective_id=0, has_side_effects=True, vmem_limit_bytes=48 * 1024 * 1024
        ),
    )(hidden, conv_weight, feat_query_w, feat_key_w, win_query, win_key, selk, selq, rowq)


def solution(mesh):
    placed = (P(("groups", "seq"), None), P(), P(), P(), P(("groups", "seq"), None), P(("groups", "seq"), None))
    return jax.shard_map(
        functools.partial(local, mesh.shape["seq"]),
        mesh=mesh, in_specs=placed, out_specs=P(("groups", "seq"), None), check_vma=False,
    )
```

time: 181 us -> 54.3 us (0.30)
  the two profiles are of different devices: /device:TPU:0 before, /device:TPU:27 now
where the time goes in v1:
time: 54.3 us; the launch traced here: 53.8 us
  Pallas kernels  44.7 us (82%)
  local copies, waits for them, and re-layouts  9.11 us (17%)
    pallas_call x1, Pallas kernels, local(): pl.pallas_call(functools.partial(kernel, n), out_shape=jax.ShapeDtypeStru...  44.7 us
    unnamed x17, local copies, waits for them, and re-layouts  9.11 us

profile of v1, /device:TPU:27, one launch (start us, length us, event | category | flops | bytes accessed | tf_op | source)
XLA Modules:
  0.0 53.8 jit_solution(2001425486782860502)
XLA Ops:
  0.0 0.0 copy-start
  0.0 1.2 %copy-done = bf16[256,2048]{1,0:T(8,128)(2,1)S(1)} copy-done((bf16[256,2048]{1,0:T(8,128)(2,1)S(1)}, bf16[256,2048]{1,0:T(8,128)(2,1)}, u32[]{:S(2)}) %copy-start) | copy-done | bytes 1048600
  1.2 0.0 copy-start.1
  1.2 1.2 %copy-done.1 = bf16[2048,256]{1,0:T(8,128)(2,1)S(1)} copy-done((bf16[2048,256]{1,0:T(8,128)(2,1)S(1)}, bf16[2048,256]{1,0:T(8,128)(2,1)}, u32[]{:S(2)}) %copy-start.1) | copy-done | bytes 1048600
  2.5 0.0 copy-start.2
  2.5 1.2 %copy-done.2 = bf16[2048,256]{1,0:T(8,128)(2,1)S(1)} copy-done((bf16[2048,256]{1,0:T(8,128)(2,1)S(1)}, bf16[2048,256]{1,0:T(8,128)(2,1)}, u32[]{:S(2)}) %copy-start.2) | copy-done | bytes 1048600
  3.7 0.0 copy-start.3
  3.7 1.2 %copy-done.3 = bf16[256,2048]{1,0:T(8,128)(2,1)S(1)} copy-done((bf16[256,2048]{1,0:T(8,128)(2,1)S(1)}, bf16[256,2048]{1,0:T(8,128)(2,1)}, u32[]{:S(2)}) %copy-start.3) | copy-done | bytes 1048600
  4.9 0.0 copy-start.4
  4.9 0.9 %copy-done.4 = bf16[128,512]{1,0:T(8,128)(2,1)S(1)} copy-done((bf16[128,512]{1,0:T(8,128)(2,1)S(1)}, bf16[128,512]{1,0:T(8,128)(2,1)}, u32[]{:S(2)}) %copy-start.4) | copy-done | bytes 131096
  5.8 0.0 copy-start.5
  5.8 0.9 %copy-done.5 = bf16[320,32]{1,0:T(8,128)(2,1)S(1)} copy-done((bf16[320,32]{1,0:T(8,128)(2,1)S(1)}, bf16[320,32]{1,0:T(8,128)(2,1)}, u32[]{:S(2)}) %copy-start.5) | copy-done | bytes 20504
  6.7 0.0 copy-start.6
  6.7 0.8 %copy-done.6 = f32[3,2048]{1,0:T(4,128)S(1)} copy-done((f32[3,2048]{1,0:T(4,128)S(1)}, f32[3,2048]{1,0:T(4,128)}, u32[]{:S(2)}) %copy-start.6) | copy-done | bytes 24600
  7.5 0.0 copy-start.7
  7.5 0.7 %copy-done.7 = f32[8,256]{1,0:T(8,128)S(1)} copy-done((f32[8,256]{1,0:T(8,128)S(1)}, f32[8,256]{1,0:T(8,128)}, u32[]{:S(2)}) %copy-start.7) | copy-done | bytes 8216
  8.1 44.7 %shard_map.91 = bf16[256,2048]{1,0:T(8,128)(2,1)S(1)} custom-call(bf16[256,2048]{1,0:T(8,128)(2,1)S(1)} %copy-done, f32[3,2048]{1,0:T(4,128)S(1)} %copy-done.6, bf16[2048,256]{1,0:T(8,128)(2,1)S(1)} %copy-done.1, bf16[2048,256]{1,0:T(8,128)(2,1)S(1)} %copy-done.2, bf16[256,2048]{1,0:T(8,128)(2,1)S(1)} %copy-done.3, bf16[256,2048]{1,0:T(8,128)(2,1)} %key.1, ...), custom_call_target="tpu_custom_call" | custom-call | tf_op jit(solution)/shard_map/pallas_call | solution.py:294
  52.9 1.0 %copy.11 = bf16[256,2048]{1,0:T(8,128)(2,1)} copy(bf16[256,2048]{1,0:T(8,128)(2,1)S(1)} %shard_map.91) | data formatting | bytes 2097152
Async XLA Ops:
  0.0 1.2 %copy-start = (bf16[256,2048]{1,0:T(8,128)(2,1)S(1)}, bf16[256,2048]{1,0:T(8,128)(2,1)}, u32[]{:S(2)}) copy-start(bf16[256,2048]{1,0:T(8,128)(2,1)} %hid.1) | copy-start | bytes 3145732
  1.2 1.2 %copy-start.1 = (bf16[2048,256]{1,0:T(8,128)(2,1)S(1)}, bf16[2048,256]{1,0:T(8,128)(2,1)}, u32[]{:S(2)}) copy-start(bf16[2048,256]{1,0:T(8,128)(2,1)} %wq.1) | copy-start | bytes 3145732
  2.5 1.2 %copy-start.2 = (bf16[2048,256]{1,0:T(8,128)(2,1)S(1)}, bf16[2048,256]{1,0:T(8,128)(2,1)}, u32[]{:S(2)}) copy-start(bf16[2048,256]{1,0:T(8,128)(2,1)} %wk.1) | copy-start | bytes 3145732
  3.7 1.2 %copy-start.3 = (bf16[256,2048]{1,0:T(8,128)(2,1)S(1)}, bf16[256,2048]{1,0:T(8,128)(2,1)}, u32[]{:S(2)}) copy-start(bf16[256,2048]{1,0:T(8,128)(2,1)} %qry.1) | copy-start | bytes 3145732
  4.9 0.9 %copy-start.4 = (bf16[128,512]{1,0:T(8,128)(2,1)S(1)}, bf16[128,512]{1,0:T(8,128)(2,1)}, u32[]{:S(2)}) copy-start(bf16[128,512]{1,0:T(8,128)(2,1)} %constant.7.clone.selq) | copy-start | bytes 393220
  5.8 0.9 %copy-start.5 = (bf16[320,32]{1,0:T(8,128)(2,1)S(1)}, bf16[320,32]{1,0:T(8,128)(2,1)}, u32[]{:S(2)}) copy-start(bf16[320,32]{1,0:T(8,128)(2,1)} %constant.6.clone.selk) | copy-start | bytes 61444
  6.7 0.8 %copy-start.6 = (f32[3,2048]{1,0:T(4,128)S(1)}, f32[3,2048]{1,0:T(4,128)}, u32[]{:S(2)}) copy-start(f32[3,2048]{1,0:T(4,128)} %cw.1) | copy-start | bytes 73732
  7.5 0.7 %copy-start.7 = (f32[8,256]{1,0:T(8,128)S(1)}, f32[8,256]{1,0:T(8,128)}, u32[]{:S(2)}) copy-start(f32[8,256]{1,0:T(8,128)} %constant.8.clone.rowq) | copy-start | bytes 24580

commit v2 on v1

--- a/solution.py
+++ b/solution.py
@@ -14,6 +14,10 @@
 TEAM = 4
 ROWS = 160
 QUADS = 136
+CHUNKS = 2
+TURN0 = 1
+TURNC = 1
+TURNT = 2
 C2 = (FEAT**-0.5) / 2.0**0.5
 BF = jnp.bfloat16
 F32 = jnp.float32
@@ -56,10 +60,11 @@
 
 
 def kernel(
-    n, hid, cw, wq, wk, qry, key, selk, selq, rowq, out,
-    hprev, kprev, vprev, cv, fqs, fkt, st, rbuf, total, cin, cout, obuf, sbuf,
+    n, hid_h, cw_h, wq_h, wk_h, qry_h, key_h, selk_h, selq_h, rowq_h, out,
+    hid, cw, wq, wk, qry, key, selk, selq, rowq,
+    hprev, kprev, vprev, cv, fqs, fkt, st, rbuf, cin, cout, obuf, sbuf,
     ywin, num, den, wbias, cmask,
-    hs_send, hs_recv, a_send, a_recv, c_send, c_recv, b_send, b_recv,
+    loads, hs_send, hs_recv, a_send, a_recv, c_send, c_recv, b_send, b_recv,
 ):
     count, width = hid.shape
     head = width // HEADS
@@ -75,6 +80,14 @@
     def peer(d):
         return base_dev + lax.rem(pos + d, TEAM)
 
+    pairs = (
+        (hid_h, hid), (cw_h, cw), (wk_h, wk), (selk_h, selk), (wq_h, wq),
+        (qry_h, qry), (key_h, key), (selq_h, selq), (rowq_h, rowq),
+    )
+    fetch = [pltpu.make_async_copy(a, b, loads.at[i]) for i, (a, b) in enumerate(pairs)]
+    for copy in fetch:
+        copy.start()
+
     barrier = pltpu.get_barrier_semaphore()
 
     def hello(dev):
@@ -97,8 +110,8 @@
             device_id={"seq": dev}, device_id_type=pl.DeviceIdType.MESH,
         )
 
-    tail_copy = remote(hid.at[pl.ds(count - 16, 16)], hprev, hs_send.at[0], hs_recv.at[0], me + 1)
-    key_copy = remote(key.at[pl.ds(count - WINDOW, WINDOW)], kprev, hs_send.at[1], hs_recv.at[1], me + 1)
+    tail_copy = remote(hid_h.at[pl.ds(count - 16, 16)], hprev, hs_send.at[0], hs_recv.at[0], me + 1)
+    key_copy = remote(key_h.at[pl.ds(count - WINDOW, WINDOW)], kprev, hs_send.at[1], hs_recv.at[1], me + 1)
     val_copy = remote(cv.at[pl.ds(count - WINDOW, WINDOW)], vprev, hs_send.at[2], hs_recv.at[2], me + 1)
 
     @pl.when(has_next)
@@ -118,16 +131,20 @@
     first = jnp.where(has_prev, 0, WINDOW)
     ok = (j > rr) & (j <= rr + WINDOW) & ((j >= first) | (r >= WINDOW))
     wbias[...] = jnp.where(ok, 0.0, -1e30)
-    r = lax.broadcasted_iota(jnp.int32, (count, count), 0)
-    j = lax.broadcasted_iota(jnp.int32, (count, count), 1)
+    half = count // 2
+    r = lax.broadcasted_iota(jnp.int32, (half, half), 0)
+    j = lax.broadcasted_iota(jnp.int32, (half, half), 1)
     cmask[...] = jnp.where(j <= r, 1.0, 0.0)
 
+    for copy in fetch[:4]:
+        copy.wait()
     pl.when(has_prev)(lambda: tail_copy.wait_recv())
 
-    row = lax.broadcasted_iota(jnp.int32, (count, head), 0)
+    wide = 2 * head
+    row = lax.broadcasted_iota(jnp.int32, (count, wide), 0)
 
     def conv_step(b, c):
-        cols = pl.ds(pl.multiple_of(b * head, head), head)
+        cols = pl.ds(pl.multiple_of(b * wide, wide), wide)
         h = hid[:, cols].astype(F32)
         hp = hprev[:, cols].astype(F32)
         w = cw[:, cols]
@@ -136,7 +153,7 @@
         cv[:, cols] = (w[0:1] * h2 + w[1:2] * h1 + w[2:3] * h).astype(BF)
         return c
 
-    lax.fori_loop(0, HEADS, conv_step, 0)
+    lax.fori_loop(0, width // wide, conv_step, 0)
     pl.when(has_next)(lambda: val_copy.start())
 
     fk = nn(cv[...], wk[...]).astype(BF).astype(F32)
@@ -148,7 +165,7 @@
     ones_k = jnp.ones((FEAT, count), BF)
     zeros_k = jnp.zeros((256 - ROWS, count), BF)
 
-    def state_step(h, c):
+    def state_step(h):
         x = jnp.concatenate([fkt[pl.ds(pl.multiple_of(h * FEAT, FEAT), FEAT), :], ones_k], axis=0)
         ab = nn(selk[...], x)
         p = ab[:ROWS] * ab[ROWS:]
@@ -157,17 +174,27 @@
         s = nn(p, v)
         tail = s[144:] + nt(pick_a, p[:128]) + nt(pick_b, jnp.concatenate([p[128:], zeros_k], axis=0))
         st[h] = jnp.concatenate([s[:144], tail], axis=0).astype(BF)
-        return c
-
-    a_copies = []
-    for d in range(1, TEAM):
-        p_d = lax.rem(pos + d, TEAM)
-        lax.fori_loop(0, per, lambda k, c, p_d=p_d: state_step(p_d * per + k, c), 0)
-        copy = remote(st.at[pl.ds(p_d * per, per)], rbuf.at[pos], a_send.at[d], a_recv.at[d], peer(d))
-        copy.start()
-        a_copies.append(copy)
-    lax.fori_loop(0, per, lambda k, c: state_step(pos * per + k, c), 0)
-
+
+    each = per // CHUNKS
+
+    def to_owner(c, d):
+        heads = pl.ds(lax.rem(pos + d, TEAM) * per + c * each, each)
+        return remote(
+            st.at[heads], rbuf.at[pos, pl.ds(c * each, each)], a_send.at[c, d], a_recv.at[c, d], peer(d)
+        )
+
+    for c in range(CHUNKS):
+
+        def for_peer(d, carry, c=c):
+            h = lax.rem(pos + d, TEAM) * per + c * each
+            for k in range(each):
+                state_step(h + k)
+            pl.when(d < TEAM)(lambda: to_owner(c, d).start())
+            return carry
+
+        lax.fori_loop(1, TEAM + 1, for_peer, 0)
+
+    fetch[4].wait()
     fq = nn(cv[...], wq[...]).astype(BF)
     for b in range(2):
         fqs[b] = fq[:, b * 128 : (b + 1) * 128]
@@ -179,7 +206,9 @@
         mask = jnp.where(lane // FEAT == lax.rem(h, 8), 1.0, 0.0)[0:1].astype(BF)
         return fqs[h // 8] * mask
 
-    def local_step(h, c):
+    lin, sq = FEAT**-0.5, 0.5 / FEAT
+
+    def local_step(h):
         cols = pl.ds(pl.multiple_of(h * head, head), head)
         q = qry[:, cols]
         k = jnp.concatenate([kprev[:, cols], key[:, cols]], axis=0)
@@ -196,67 +225,78 @@
         )
         ywin[:, cols] = y[:, :head] / y[:, head:]
         fqm = masked_query(h)
-        x = nn(fqm, fkt[pl.ds(pl.multiple_of((h // 8) * 128, 128), 128), :]) * FEAT**-0.5
-        a = ((1.0 + x + 0.5 * x * x) * cmask[...]).astype(BF)
-        na = nn(a, jnp.concatenate([v, ones_v], axis=1))
-        num[:, cols] = na[:, :head]
-        den[:, cols] = na[:, head:]
-        return c
-
-    def collect():
-        rbuf[pos] = st[pl.ds(pos * per, per)]
-        for copy in a_copies:
-            copy.wait_recv()
-        total[...] = (
-            rbuf[0].astype(F32) + rbuf[1].astype(F32) + rbuf[2].astype(F32) + rbuf[3].astype(F32)
-        )
-
-    chain = remote(cout, cin, c_send, c_recv, me + TEAM)
-    b_copies = [
-        remote(obuf.at[d], sbuf.at[pos], b_send.at[d], b_recv.at[d], peer(d)) for d in range(1, TEAM)
-    ]
-
-    def pass_on():
-        pl.when(has_up)(lambda: chain.wait_recv())
+        kt = fkt[pl.ds(pl.multiple_of((h // 8) * 128, 128), 128), :]
+        vb = jnp.concatenate([v, ones_v], axis=1)
+        x = nn(fqm[:half], kt[:, :half])
+        a = ((1.0 + x * (lin + sq * x)) * cmask[...]).astype(BF)
+        na = nn(a, vb[:half])
+        num[:half, cols] = na[:, :head]
+        den[:half, cols] = na[:, head:]
+        x = nn(fqm[half:], kt)
+        a = 1.0 + x * (lin + sq * x)
+        a = jnp.concatenate([a[:, :half], a[:, half:] * cmask[...]], axis=1).astype(BF)
+        na = nn(a, vb)
+        num[half:, cols] = na[:, :head]
+        den[half:, cols] = na[:, head:]
+
+    def chain(c):
+        part = pl.ds(c * each, each)
+        return remote(cout.at[part], cin.at[part], c_send.at[c], c_recv.at[c], me + TEAM)
+
+    def to_user(c, d):
+        part = pl.ds(c * each, each)
+        return remote(obuf.at[d, part], sbuf.at[pos, part], b_send.at[c, d], b_recv.at[c, d], peer(d))
+
+    def pass_on(c):
+        part = pl.ds(c * each, each)
+        rbuf[pos, part] = st[pl.ds(pos * per + c * each, each)]
+        for d in range(1, TEAM):
+            to_owner(c, d).wait_recv()
+        got = [rbuf[i, part].astype(F32) for i in range(TEAM)]
+        pl.when(has_up)(lambda: chain(c).wait_recv())
 
         @pl.when(jnp.logical_not(has_up))
         def _():
-            cin[...] = jnp.zeros_like(cin)
+            cin[part] = jnp.zeros_like(cin[part])
+
+        base = cin[part].astype(F32)
 
         @pl.when(has_down)
         def _():
-            cout[...] = (cin[...].astype(F32) + total[...]).astype(BF)
-            chain.start()
-
-        base = cin[...].astype(F32)
-        for d in range(TEAM):
+            cout[part] = (base + (got[0] + got[1] + got[2] + got[3])).astype(BF)
+            chain(c).start()
+
+        for d in (2, 3, 1, 0):
             target = lax.rem(pos + d, TEAM)
             acc = base
             for i in range(TEAM - 1):
-                acc = acc + rbuf[i].astype(F32) * jnp.where(i < target, 1.0, 0.0)
+                acc = acc + got[i] * jnp.where(i < target, 1.0, 0.0)
             if d == 0:
-                sbuf[pos] = acc.astype(BF)
+                sbuf[pos, part] = acc.astype(BF)
             else:
-                obuf[d] = acc.astype(BF)
-                b_copies[d - 1].start()
-
+                obuf[d, part] = acc.astype(BF)
+                to_user(c, d).start()
+
+    for copy in fetch[5:]:
+        copy.wait()
     pl.when(has_prev)(lambda: key_copy.wait_recv())
     pl.when(has_prev)(lambda: val_copy.wait_recv())
-    lax.fori_loop(0, 4, local_step, 0)
-    collect()
-    turn = jnp.minimum(4 + 4 * team, HEADS - 1)
-
-    def local_and_pass(h, c):
-        pl.when(h == turn)(pass_on)
-        return local_step(h, c)
-
-    lax.fori_loop(4, HEADS, local_and_pass, 0)
-    for copy in b_copies:
-        copy.wait_recv()
+
+    steps = HEADS // 2
+    turns = [jnp.minimum(TURN0 + TURNC * c + TURNT * team, steps) for c in range(CHUNKS)]
+
+    def local_and_pass(i, carry):
+        for c in range(CHUNKS):
+            pl.when(i == turns[c])(functools.partial(pass_on, c))
+        local_step(2 * i)
+        local_step(2 * i + 1)
+        return carry
+
+    lax.fori_loop(0, steps, local_and_pass, 0)
 
     spare = jnp.zeros((256 - ROWS, head), BF)
 
-    def final_step(h, c):
+    def final_step(h):
         cols = pl.ds(pl.multiple_of(h * head, head), head)
         lr = nn(masked_query(h), selq[...])
         ph = (((lr[:, :256] + rowq[0:1]) * (lr[:, 256:] + rowq[1:2])) * rowq[2:3]).astype(BF)
@@ -269,9 +309,23 @@
         do = nt(ph, nrow)
         y = ywin[:, cols] + (num[:, cols] + no) / (den[:, cols] + do)
         out[:, cols] = y.astype(BF)
-        return c
-
-    lax.fori_loop(0, HEADS, final_step, 0)
+
+    def finish(c, d):
+        h = lax.rem(pos + TEAM - d, TEAM) * per + c * each
+        for k in range(each):
+            final_step(h + k)
+
+    for c in range(CHUNKS):
+        pl.when(turns[c] == steps)(functools.partial(pass_on, c))
+        finish(c, 0)
+    for c in range(CHUNKS):
+
+        def from_owner(d, carry, c=c):
+            to_user(c, d).wait_recv()
+            finish(c, d)
+            return carry
+
+        lax.fori_loop(1, TEAM, from_owner, 0)
 
     @pl.when(has_next)
     def _():
@@ -279,9 +333,11 @@
         key_copy.wait_send()
         val_copy.wait_send()
 
-    for copy in a_copies + b_copies:
-        copy.wait_send()
-    pl.when(has_down)(lambda: chain.wait_send())
+    for c in range(CHUNKS):
+        for d in range(1, TEAM):
+            to_owner(c, d).wait_send()
+            to_user(c, d).wait_send()
+        pl.when(has_down)(lambda c=c: chain(c).wait_send())
 
 
 def local(n, hidden, conv_weight, feat_query_w, feat_key_w, win_query, win_key):
@@ -294,9 +350,18 @@
     return pl.pallas_call(
         functools.partial(kernel, n),
         out_shape=jax.ShapeDtypeStruct((count, width), BF),
-        in_specs=[pl.BlockSpec(memory_space=pltpu.VMEM)] * 9,
+        in_specs=[pl.BlockSpec(memory_space=pl.ANY)] * 9,
         out_specs=pl.BlockSpec(memory_space=pltpu.VMEM),
         scratch_shapes=[
+            pltpu.VMEM((count, width), BF),
+            pltpu.VMEM(conv_weight.shape, F32),
+            pltpu.VMEM(feat_query_w.shape, BF),
+            pltpu.VMEM(feat_key_w.shape, BF),
+            pltpu.VMEM((count, width), BF),
+            pltpu.VMEM((count, width), BF),
+            pltpu.VMEM(selk.shape, BF),
+            pltpu.VMEM(selq.shape, BF),
+            pltpu.VMEM(rowq.shape, F32),
             pltpu.VMEM((16, width), BF),
             pltpu.VMEM((WINDOW, width), BF),
             pltpu.VMEM((WINDOW, width), BF),
@@ -305,7 +370,6 @@
             pltpu.VMEM((256, count), BF),
             pltpu.VMEM((HEADS, ROWS, head), BF),
             pltpu.VMEM((TEAM,) + quarter, BF),
-            pltpu.VMEM(quarter, F32),
             pltpu.VMEM(quarter, BF),
             pltpu.VMEM(quarter, BF),
             pltpu.VMEM((TEAM,) + quarter, BF),
@@ -314,11 +378,12 @@
             pltpu.VMEM((count, width), F32),
             pltpu.VMEM((count, width), F32),
             pltpu.VMEM((count, head), F32),
-            pltpu.VMEM((count, count), F32),
-            dma((3,)), dma((3,)), dma((TEAM,)), dma((TEAM,)), dma, dma, dma((TEAM,)), dma((TEAM,)),
+            pltpu.VMEM((count // 2, count // 2), F32),
+            dma((9,)), dma((3,)), dma((3,)), dma((CHUNKS, TEAM)), dma((CHUNKS, TEAM)),
+            dma((CHUNKS,)), dma((CHUNKS,)), dma((CHUNKS, TEAM)), dma((CHUNKS, TEAM)),
         ],
         compiler_params=pltpu.CompilerParams(
-            collective_id=0, has_side_effects=True, vmem_limit_bytes=48 * 1024 * 1024
+            collective_id=0, has_side_effects=True, vmem_limit_bytes=56 * 1024 * 1024
         ),
     )(hidden, conv_weight, feat_query_w, feat_key_w, win_query, win_key, selk, selq, rowq)
 

time: 54.3 us -> 38.3 us (0.71)
  Pallas kernels: 44.7 us -> 35.8 us
  local copies, waits for them, and re-layouts: 9.11 us -> 2.3 us
    pallas_call x1, Pallas kernels: 44.7 us -> 35.8 us  [local(): pl.pallas_call(functools.partial(kernel, n), out_shape=jax.ShapeDtypeStru...]
    unnamed x17 -> x1, local copies, waits for them, and re-layouts: 9.11 us -> 2.3 us
where the time goes in v2:
time: 38.3 us; the launch traced here: 38.1 us
  Pallas kernels  35.8 us (93%)
  local copies, waits for them, and re-layouts  2.3 us (6%)
    pallas_call x1, Pallas kernels, local(): pl.pallas_call(functools.partial(kernel, n), out_shape=jax.ShapeDtypeStru...  35.8 us
    unnamed x1, local copies, waits for them, and re-layouts  2.3 us

profile of v2, /device:TPU:27, one launch (start us, length us, event | category | flops | bytes accessed | tf_op | source)
XLA Modules:
  0.0 38.1 jit_solution(11598132450950276351)
XLA Ops:
  0.0 35.8 %shard_map.91 = bf16[256,2048]{1,0:T(8,128)(2,1)} custom-call(bf16[256,2048]{1,0:T(8,128)(2,1)} %hid_h.1, f32[3,2048]{1,0:T(4,128)} %cw_h.1, bf16[2048,256]{1,0:T(8,128)(2,1)} %wq_h.1, bf16[2048,256]{1,0:T(8,128)(2,1)} %wk_h.1, bf16[256,2048]{1,0:T(8,128)(2,1)} %qry_h.1, bf16[256,2048]{1,0:T(8,128)(2,1)} %key_h.1, bf16[320,32]{1,0:T(8,128)(2,1)} %constant.6.clone.selk_h, ...), custom_call_target="tpu_custom_call" | custom-call | tf_op jit(solution)/shard_map/pallas_call | solution.py:350
  35.8 2.3 %copy.11 = bf16[256,2048]{1,0:T(8,128)(2,1)} copy(bf16[256,2048]{1,0:T(8,128)(2,1)} %shard_map.91) | data formatting | bytes 2097152

commit v3 on v2

--- a/solution.py
+++ b/solution.py
@@ -12,12 +12,18 @@
 FEAT = 16
 WINDOW = 64
 TEAM = 4
+CORES = 2
+HALF = HEADS // CORES
 ROWS = 160
 QUADS = 136
-CHUNKS = 2
-TURN0 = 1
+CHUNKS = 4
+PART = HALF // CHUNKS
+TURN0 = 0
 TURNC = 1
 TURNT = 2
+TURNB = 2
+LAG = 3
+LAGB = 1
 C2 = (FEAT**-0.5) / 2.0**0.5
 BF = jnp.bfloat16
 F32 = jnp.float32
@@ -62,23 +68,22 @@
 def kernel(
     n, hid_h, cw_h, wq_h, wk_h, qry_h, key_h, selk_h, selq_h, rowq_h, out,
     hid, cw, wq, wk, qry, key, selk, selq, rowq,
-    hprev, kprev, vprev, cv, fqs, fkt, st, rbuf, cin, cout, obuf, sbuf,
+    hprev, kprev, vprev, cv, fqs, fkt, st, rbuf, cin, cout, yin, obuf, sbuf,
     ywin, num, den, wbias, cmask,
-    loads, hs_send, hs_recv, a_send, a_recv, c_send, c_recv, b_send, b_recv,
+    loads, hs_send, hs_recv, a_send, a_recv, c_send, c_recv, y_send, y_recv, b_send, b_recv,
 ):
     count, width = hid.shape
     head = width // HEADS
-    per = HEADS // TEAM
     me = lax.axis_index("seq")
     team = me // TEAM
-    pos = lax.rem(me, TEAM)
+    core = lax.rem(me, CORES)
+    side = lax.rem(me // CORES, 2)
     teams = n // TEAM
     has_prev, has_next = me > 0, me < n - 1
     has_up, has_down = team > 0, team < teams - 1
-    base_dev = team * TEAM
-
-    def peer(d):
-        return base_dev + lax.rem(pos + d, TEAM)
+    sibling = me + 1 - 2 * core
+    across = me + CORES - 2 * CORES * side
+    mine_at, theirs_at = core * HALF, (1 - core) * HALF
 
     pairs = (
         (hid_h, hid), (cw_h, cw), (wk_h, wk), (selk_h, selk), (wq_h, wq),
@@ -93,13 +98,13 @@
     def hello(dev):
         pl.semaphore_signal(barrier, inc=1, device_id={"seq": dev}, device_id_type=pl.DeviceIdType.MESH)
 
-    for d in range(1, TEAM):
-        hello(peer(d))
+    hello(sibling)
+    hello(across)
     pl.when(has_prev)(lambda: hello(me - 1))
     pl.when(has_next)(lambda: hello(me + 1))
     pl.when(has_up)(lambda: hello(me - TEAM))
     pl.when(has_down)(lambda: hello(me + TEAM))
-    greeted = TEAM - 1
+    greeted = 2
     for there in (has_prev, has_next, has_up, has_down):
         greeted = greeted + there.astype(jnp.int32)
     pl.semaphore_wait(barrier, greeted)
@@ -175,24 +180,21 @@
         tail = s[144:] + nt(pick_a, p[:128]) + nt(pick_b, jnp.concatenate([p[128:], zeros_k], axis=0))
         st[h] = jnp.concatenate([s[:144], tail], axis=0).astype(BF)
 
-    each = per // CHUNKS
-
-    def to_owner(c, d):
-        heads = pl.ds(lax.rem(pos + d, TEAM) * per + c * each, each)
+    def to_sibling(k):
         return remote(
-            st.at[heads], rbuf.at[pos, pl.ds(c * each, each)], a_send.at[c, d], a_recv.at[c, d], peer(d)
+            st.at[pl.ds(theirs_at + k * PART, PART)], rbuf.at[pl.ds(k * PART, PART)],
+            a_send.at[k], a_recv.at[k], sibling,
         )
 
-    for c in range(CHUNKS):
-
-        def for_peer(d, carry, c=c):
-            h = lax.rem(pos + d, TEAM) * per + c * each
-            for k in range(each):
-                state_step(h + k)
-            pl.when(d < TEAM)(lambda: to_owner(c, d).start())
-            return carry
-
-        lax.fori_loop(1, TEAM + 1, for_peer, 0)
+    def states(k, carry):
+        for i in range(PART):
+            state_step(theirs_at + k * PART + i)
+        to_sibling(k).start()
+        for i in range(PART):
+            state_step(mine_at + k * PART + i)
+        return carry
+
+    lax.fori_loop(0, CHUNKS, states, 0)
 
     fetch[4].wait()
     fq = nn(cv[...], wq[...]).astype(BF)
@@ -239,43 +241,45 @@
         num[half:, cols] = na[:, :head]
         den[half:, cols] = na[:, head:]
 
-    def chain(c):
-        part = pl.ds(c * each, each)
-        return remote(cout.at[part], cin.at[part], c_send.at[c], c_recv.at[c], me + TEAM)
-
-    def to_user(c, d):
-        part = pl.ds(c * each, each)
-        return remote(obuf.at[d, part], sbuf.at[pos, part], b_send.at[c, d], b_recv.at[c, d], peer(d))
-
-    def pass_on(c):
-        part = pl.ds(c * each, each)
-        rbuf[pos, part] = st[pl.ds(pos * per + c * each, each)]
-        for d in range(1, TEAM):
-            to_owner(c, d).wait_recv()
-        got = [rbuf[i, part].astype(F32) for i in range(TEAM)]
-        pl.when(has_up)(lambda: chain(c).wait_recv())
+    def chain(k):
+        part = pl.ds(k * PART, PART)
+        return remote(cout.at[part], cin.at[part], c_send.at[k], c_recv.at[k], me + TEAM)
+
+    def cross(k, src):
+        part = pl.ds(k * PART, PART)
+        return remote(src.at[part], yin.at[part], y_send.at[k], y_recv.at[k], across)
+
+    def back(k):
+        return remote(
+            obuf.at[pl.ds(k * PART, PART)], sbuf.at[pl.ds(mine_at + k * PART, PART)],
+            b_send.at[k], b_recv.at[k], sibling,
+        )
+
+    def pass_on(k):
+        part = pl.ds(k * PART, PART)
+        to_sibling(k).wait_recv()
+        both = st[pl.ds(mine_at + k * PART, PART)].astype(F32) + rbuf[part].astype(F32)
+        pl.when(has_up)(lambda: chain(k).wait_recv())
 
         @pl.when(jnp.logical_not(has_up))
         def _():
             cin[part] = jnp.zeros_like(cin[part])
 
-        base = cin[part].astype(F32)
-
-        @pl.when(has_down)
-        def _():
-            cout[part] = (base + (got[0] + got[1] + got[2] + got[3])).astype(BF)
-            chain(c).start()
-
-        for d in (2, 3, 1, 0):
-            target = lax.rem(pos + d, TEAM)
-            acc = base
-            for i in range(TEAM - 1):
-                acc = acc + got[i] * jnp.where(i < target, 1.0, 0.0)
-            if d == 0:
-                sbuf[pos, part] = acc.astype(BF)
-            else:
-                obuf[d, part] = acc.astype(BF)
-                to_user(c, d).start()
+        cout[part] = (cin[part].astype(F32) + both).astype(BF)
+        pl.when(has_down)(lambda: chain(k).start())
+        pl.when(side == 0)(lambda: cross(k, cout).start())
+        pl.when(side == 1)(lambda: cross(k, cin).start())
+
+    own_first = jnp.where(core == 0, 1.0, 0.0)
+
+    def give_back(k):
+        part = pl.ds(k * PART, PART)
+        cross(k, cin).wait_recv()
+        before = cin[part].astype(F32) + yin[part].astype(F32)
+        at = pl.ds(mine_at + k * PART, PART)
+        obuf[part] = (before + own_first * st[at].astype(F32)).astype(BF)
+        back(k).start()
+        sbuf[at] = (before + (1.0 - own_first) * rbuf[part].astype(F32)).astype(BF)
 
     for copy in fetch[5:]:
         copy.wait()
@@ -283,11 +287,22 @@
     pl.when(has_prev)(lambda: val_copy.wait_recv())
 
     steps = HEADS // 2
-    turns = [jnp.minimum(TURN0 + TURNC * c + TURNT * team, steps) for c in range(CHUNKS)]
+    def turn(k):
+        return jnp.minimum(TURN0 + TURNC * k + TURNT * team, steps)
+
+    def turn_back(k):
+        return jnp.minimum(turn(k) + TURNB, steps)
+
+    def events(i):
+        def one(k, carry):
+            pl.when(i == turn(k))(lambda: pass_on(k))
+            pl.when(i == turn_back(k))(lambda: give_back(k))
+            return carry
+
+        lax.fori_loop(0, CHUNKS, one, 0)
 
     def local_and_pass(i, carry):
-        for c in range(CHUNKS):
-            pl.when(i == turns[c])(functools.partial(pass_on, c))
+        events(i)
         local_step(2 * i)
         local_step(2 * i + 1)
         return carry
@@ -300,7 +315,7 @@
         cols = pl.ds(pl.multiple_of(h * head, head), head)
         lr = nn(masked_query(h), selq[...])
         ph = (((lr[:, :256] + rowq[0:1]) * (lr[:, 256:] + rowq[1:2])) * rowq[2:3]).astype(BF)
-        s = sbuf[h // per, lax.rem(h, per)]
+        s = sbuf[h]
         t = s[144:].astype(F32)
         nrow = jnp.concatenate(
             [jnp.broadcast_to(t[9:10], (head, head)), jnp.broadcast_to(t[10:11], (head, head))], axis=1
@@ -310,22 +325,26 @@
         y = ywin[:, cols] + (num[:, cols] + no) / (den[:, cols] + do)
         out[:, cols] = y.astype(BF)
 
-    def finish(c, d):
-        h = lax.rem(pos + TEAM - d, TEAM) * per + c * each
-        for k in range(each):
-            final_step(h + k)
-
-    for c in range(CHUNKS):
-        pl.when(turns[c] == steps)(functools.partial(pass_on, c))
-        finish(c, 0)
-    for c in range(CHUNKS):
-
-        def from_owner(d, carry, c=c):
-            to_user(c, d).wait_recv()
-            finish(c, d)
-            return carry
-
-        lax.fori_loop(1, TEAM, from_owner, 0)
+    def wind_up(k, carry):
+        @pl.when(k < CHUNKS)
+        def _():
+            pl.when(turn(k) == steps)(lambda: pass_on(k))
+
+        @pl.when((k >= LAG) & (k < CHUNKS + LAG))
+        def _():
+            pl.when(turn_back(k - LAG) == steps)(lambda: give_back(k - LAG))
+            for i in range(PART):
+                final_step(mine_at + (k - LAG) * PART + i)
+
+        @pl.when(k >= LAG + LAGB)
+        def _():
+            back(k - LAG - LAGB).wait_recv()
+            for i in range(PART):
+                final_step(theirs_at + (k - LAG - LAGB) * PART + i)
+
+        return carry
+
+    lax.fori_loop(0, CHUNKS + LAG + LAGB, wind_up, 0)
 
     @pl.when(has_next)
     def _():
@@ -333,19 +352,18 @@
         key_copy.wait_send()
         val_copy.wait_send()
 
-    for c in range(CHUNKS):
-        for d in range(1, TEAM):
-            to_owner(c, d).wait_send()
-            to_user(c, d).wait_send()
-        pl.when(has_down)(lambda c=c: chain(c).wait_send())
+    for k in range(CHUNKS):
+        to_sibling(k).wait_send()
+        cross(k, cin).wait_send()
+        back(k).wait_send()
+        pl.when(has_down)(lambda k=k: chain(k).wait_send())
 
 
 def local(n, hidden, conv_weight, feat_query_w, feat_key_w, win_query, win_key):
     count, width = hidden.shape
     head = width // HEADS
-    per = HEADS // TEAM
     selk, selq, rowq = tables(128)
-    quarter = (per, ROWS, head)
+    half = (HALF, ROWS, head)
     dma = pltpu.SemaphoreType.DMA
     return pl.pallas_call(
         functools.partial(kernel, n),
@@ -369,19 +387,20 @@
             pltpu.VMEM((2, count, 128), BF),
             pltpu.VMEM((256, count), BF),
             pltpu.VMEM((HEADS, ROWS, head), BF),
-            pltpu.VMEM((TEAM,) + quarter, BF),
-            pltpu.VMEM(quarter, BF),
-            pltpu.VMEM(quarter, BF),
-            pltpu.VMEM((TEAM,) + quarter, BF),
-            pltpu.VMEM((TEAM,) + quarter, BF),
+            pltpu.VMEM(half, BF),
+            pltpu.VMEM(half, BF),
+            pltpu.VMEM(half, BF),
+            pltpu.VMEM(half, BF),
+            pltpu.VMEM(half, BF),
+            pltpu.VMEM((HEADS, ROWS, head), BF),
             pltpu.VMEM((count, width), F32),
             pltpu.VMEM((count, width), F32),
             pltpu.VMEM((count, width), F32),
             pltpu.VMEM((count, head), F32),
             pltpu.VMEM((count // 2, count // 2), F32),
-            dma((9,)), dma((3,)), dma((3,)), dma((CHUNKS, TEAM)), dma((CHUNKS, TEAM)),
-            dma((CHUNKS,)), dma((CHUNKS,)), dma((CHUNKS, TEAM)), dma((CHUNKS, TEAM)),
-        ],
+            dma((9,)), dma((3,)), dma((3,)),
+        ]
+        + [dma((CHUNKS,))] * 8,
         compiler_params=pltpu.CompilerParams(
             collective_id=0, has_side_effects=True, vmem_limit_bytes=56 * 1024 * 1024
         ),

time: 38.3 us -> 35.3 us (0.922)
  Pallas kernels: 35.8 us -> 32.8 us
    pallas_call x1, Pallas kernels: 35.8 us -> 32.8 us  [local(): pl.pallas_call(functools.partial(kernel, n), out_shape=jax.ShapeDtypeStru...]
where the time goes in v3:
time: 35.3 us; the launch traced here: 35.2 us
  Pallas kernels  32.8 us (93%)
  local copies, waits for them, and re-layouts  2.3 us (7%)
    pallas_call x1, Pallas kernels, local(): pl.pallas_call(functools.partial(kernel, n), out_shape=jax.ShapeDtypeStru...  32.8 us
    unnamed x1, local copies, waits for them, and re-layouts  2.3 us

profile of v3, /device:TPU:27, one launch (start us, length us, event | category | flops | bytes accessed | tf_op | source)
XLA Modules:
  0.0 35.2 jit_solution(2608576140046020243)
XLA Ops:
  0.0 32.8 %shard_map.91 = bf16[256,2048]{1,0:T(8,128)(2,1)} custom-call(bf16[256,2048]{1,0:T(8,128)(2,1)} %hid_h.1, f32[3,2048]{1,0:T(4,128)} %cw_h.1, bf16[2048,256]{1,0:T(8,128)(2,1)} %wq_h.1, bf16[2048,256]{1,0:T(8,128)(2,1)} %wk_h.1, bf16[256,2048]{1,0:T(8,128)(2,1)} %qry_h.1, bf16[256,2048]{1,0:T(8,128)(2,1)} %key_h.1, bf16[320,32]{1,0:T(8,128)(2,1)} %constant.6.clone.selk_h, ...), custom_call_target="tpu_custom_call" | custom-call | tf_op jit(solution)/shard_map/pallas_call | solution.py:368
  32.9 2.3 %copy.11 = bf16[256,2048]{1,0:T(8,128)(2,1)} copy(bf16[256,2048]{1,0:T(8,128)(2,1)} %shard_map.91) | data formatting | bytes 2097152

commit v4 on v3

--- a/solution.py
+++ b/solution.py
@@ -18,7 +18,7 @@
 QUADS = 136
 CHUNKS = 4
 PART = HALF // CHUNKS
-TURN0 = 0
+TURN0 = -1
 TURNC = 1
 TURNT = 2
 TURNB = 2
@@ -186,12 +186,42 @@
             a_send.at[k], a_recv.at[k], sibling,
         )
 
+    def chain(k):
+        part = pl.ds(k * PART, PART)
+        return remote(cout.at[part], cin.at[part], c_send.at[k], c_recv.at[k], me + TEAM)
+
+    def cross(k, src):
+        part = pl.ds(k * PART, PART)
+        return remote(src.at[part], yin.at[part], y_send.at[k], y_recv.at[k], across)
+
+    def back(k):
+        return remote(
+            obuf.at[pl.ds(k * PART, PART)], sbuf.at[pl.ds(mine_at + k * PART, PART)],
+            b_send.at[k], b_recv.at[k], sibling,
+        )
+
+    def pass_on(k):
+        part = pl.ds(k * PART, PART)
+        to_sibling(k).wait_recv()
+        both = st[pl.ds(mine_at + k * PART, PART)].astype(F32) + rbuf[part].astype(F32)
+        pl.when(has_up)(lambda: chain(k).wait_recv())
+
+        @pl.when(jnp.logical_not(has_up))
+        def _():
+            cin[part] = jnp.zeros_like(cin[part])
+
+        cout[part] = (cin[part].astype(F32) + both).astype(BF)
+        pl.when(has_down)(lambda: chain(k).start())
+        pl.when(side == 0)(lambda: cross(k, cout).start())
+        pl.when(side == 1)(lambda: cross(k, cin).start())
+
     def states(k, carry):
         for i in range(PART):
             state_step(theirs_at + k * PART + i)
         to_sibling(k).start()
         for i in range(PART):
             state_step(mine_at + k * PART + i)
+        pl.when(jnp.logical_not(has_up) & (k >= 1))(lambda: pass_on(k - 1))
         return carry
 
     lax.fori_loop(0, CHUNKS, states, 0)
@@ -200,6 +230,7 @@
     fq = nn(cv[...], wq[...]).astype(BF)
     for b in range(2):
         fqs[b] = fq[:, b * 128 : (b + 1) * 128]
+    pl.when(jnp.logical_not(has_up))(lambda: pass_on(CHUNKS - 1))
 
     ones_v = jnp.ones((count, head), BF)
     lane = lax.broadcasted_iota(jnp.int32, (8, 128), 1)
@@ -241,35 +272,6 @@
         num[half:, cols] = na[:, :head]
         den[half:, cols] = na[:, head:]
 
-    def chain(k):
-        part = pl.ds(k * PART, PART)
-        return remote(cout.at[part], cin.at[part], c_send.at[k], c_recv.at[k], me + TEAM)
-
-    def cross(k, src):
-        part = pl.ds(k * PART, PART)
-        return remote(src.at[part], yin.at[part], y_send.at[k], y_recv.at[k], across)
-
-    def back(k):
-        return remote(
-            obuf.at[pl.ds(k * PART, PART)], sbuf.at[pl.ds(mine_at + k * PART, PART)],
-            b_send.at[k], b_recv.at[k], sibling,
-        )
-
-    def pass_on(k):
-        part = pl.ds(k * PART, PART)
-        to_sibling(k).wait_recv()
-        both = st[pl.ds(mine_at + k * PART, PART)].astype(F32) + rbuf[part].astype(F32)
-        pl.when(has_up)(lambda: chain(k).wait_recv())
-
-        @pl.when(jnp.logical_not(has_up))
-        def _():
-            cin[part] = jnp.zeros_like(cin[part])
-
-        cout[part] = (cin[part].astype(F32) + both).astype(BF)
-        pl.when(has_down)(lambda: chain(k).start())
-        pl.when(side == 0)(lambda: cross(k, cout).start())
-        pl.when(side == 1)(lambda: cross(k, cin).start())
-
     own_first = jnp.where(core == 0, 1.0, 0.0)
 
     def give_back(k):
@@ -288,10 +290,10 @@
 
     steps = HEADS // 2
     def turn(k):
-        return jnp.minimum(TURN0 + TURNC * k + TURNT * team, steps)
+        return jnp.where(has_up, jnp.minimum(TURN0 + TURNC * k + TURNT * team, steps), -1)
 
     def turn_back(k):
-        return jnp.minimum(turn(k) + TURNB, steps)
+        return jnp.minimum(TURN0 + TURNC * k + TURNT * team + TURNB, steps)
 
     def events(i):
         def one(k, carry):
@@ -367,7 +369,7 @@
     dma = pltpu.SemaphoreType.DMA
     return pl.pallas_call(
         functools.partial(kernel, n),
-        out_shape=jax.ShapeDtypeStruct((count, width), BF),
+        out_shape=pltpu.VMEM((count, width), BF),
         in_specs=[pl.BlockSpec(memory_space=pl.ANY)] * 9,
         out_specs=pl.BlockSpec(memory_space=pltpu.VMEM),
         scratch_shapes=[

time: 35.3 us -> 31.4 us (0.89)
  Pallas kernels: 32.8 us -> 30.2 us
  local copies, waits for them, and re-layouts: 2.3 us -> 0.97 us
    pallas_call x1, Pallas kernels: 32.8 us -> 30.2 us  [local(): pl.pallas_call(functools.partial(kernel, n), out_shape=pltpu.VMEM((count,...]
    unnamed x1, local copies, waits for them, and re-layouts: 2.3 us -> 0.97 us
where the time goes in v4:
time: 31.4 us; the launch traced here: 31.2 us
  Pallas kernels  30.2 us (96%)
  local copies, waits for them, and re-layouts  0.97 us (3%)
    pallas_call x1, Pallas kernels, local(): pl.pallas_call(functools.partial(kernel, n), out_shape=pltpu.VMEM((count,...  30.2 us
    unnamed x1, local copies, waits for them, and re-layouts  0.97 us

profile of v4, /device:TPU:27, one launch (start us, length us, event | category | flops | bytes accessed | tf_op | source)
XLA Modules:
  0.0 31.2 jit_solution(4635926919023462523)
XLA Ops:
  0.0 30.2 %shard_map.91 = bf16[256,2048]{1,0:T(8,128)(2,1)S(1)} custom-call(bf16[256,2048]{1,0:T(8,128)(2,1)} %hid_h.1, f32[3,2048]{1,0:T(4,128)} %cw_h.1, bf16[2048,256]{1,0:T(8,128)(2,1)} %wq_h.1, bf16[2048,256]{1,0:T(8,128)(2,1)} %wk_h.1, bf16[256,2048]{1,0:T(8,128)(2,1)} %qry_h.1, bf16[256,2048]{1,0:T(8,128)(2,1)} %key_h.1, bf16[320,32]{1,0:T(8,128)(2,1)} %constant.6.clone.selk_h, ...), custom_call_target="tpu_custom_call" | custom-call | tf_op jit(solution)/shard_map/pallas_call | solution.py:370
  30.2 1.0 %copy.11 = bf16[256,2048]{1,0:T(8,128)(2,1)} copy(bf16[256,2048]{1,0:T(8,128)(2,1)S(1)} %shard_map.91) | data formatting | bytes 2097152
